TPU v7x, 512 devices: a whole 4x4x16 slice. The times are simulated.
512 devices in a mesh: dp: 8 (over x, z_hi), row: 8 (over y, core), col: 8 (over z_lo).
Axes of the slice: x: 4, y: 4, z: 16 (z_hi: 2, z_lo: 8; z = z_hi * 8 + z_lo), core: 2. Of those that a mesh axis runs over, the one named last changes fastest.
Arguments:
- inputs: bfloat16 [8, 1024, 4096], P('dp', 'col', 'row'), may hold values from -6 to 6
- weights: bfloat16 [4096, 3, 4096], P('row', None, 'col'), may hold values from -0.09375 to 0.09375
- feature_taps: float32 [3, 3, 4096], P(None, None, 'col'), may hold values from -2.5 to 2.5
- inner_taps: float32 [7, 4096], P(None, 'col'), may hold values from -2.5 to 2.5
- grad_out: bfloat16 [8, 1024, 4096], P('dp', 'row', 'col'), may hold values from -6 to 6
Outputs:
- grad_in: bfloat16 [8, 1024, 4096], P('dp', 'col', 'row')
- grad_weights: float32 [4096, 3, 4096], P('row', None, 'col')
All inputs are finite; a program needn't handle non-finite values.
Results may differ from a plain program's by a relative error of at most 0.033.
Values may be sent and summed in bfloat16 or wider, within the bound.
A program may use at most 64 MiB of HBM per device.

v0:
```python
import jax
import jax.numpy as jnp
from jax import lax
from jax.sharding import PartitionSpec as P


def with_halo(cells, sides, width):
    for axis, dim in sides:
        count = lax.axis_size(axis)
        ends = count - 1
        head = lax.slice_in_dim(cells, 0, width, axis=dim)
        tail = lax.slice_in_dim(cells, cells.shape[dim] - width, cells.shape[dim], axis=dim)
        cells = jnp.concatenate(
            [
                lax.ppermute(tail, axis, [(i, (i + 1) % count) for i in range(ends)]),
                cells,
                lax.ppermute(head, axis, [((i + 1) % count, i) for i in range(ends)]),
            ],
            axis=dim,
        )
    return cells


def shifted(shard, axis, by):
    length = lax.axis_size(axis)
    pairs = [(i, i + by) for i in range(length) if 0 <= i + by < length]
    return lax.ppermute(shard, axis, pairs)


def causal(seq, taps):
    total = taps[0] * seq
    for lag in range(1, taps.shape[0]):
        pad = jnp.zeros((lag,) + seq.shape[1:], jnp.float32)
        total = total + taps[lag] * jnp.concatenate([pad, seq[:-lag]], axis=0)
    return total


def anticausal(seq, taps):
    total = taps[0] * seq
    for lag in range(1, taps.shape[0]):
        pad = jnp.zeros((lag,) + seq.shape[1:], jnp.float32)
        total = total + taps[lag] * jnp.concatenate([seq[lag:], pad], axis=0)
    return total


def rounded(value):
    return lax.optimization_barrier(value.astype(jnp.bfloat16)).astype(jnp.float32)


def on_device(inputs, weights, feature_taps, inner_taps, grad_out):
    tile = inputs[0]
    upstream_tile = grad_out[0]
    rows_dev = upstream_tile.shape[0]
    width_row = weights.shape[0]
    width_col = weights.shape[2]
    margin = feature_taps.shape[0] - 1 + (inner_taps.shape[0] - 1)
    flat_w = weights.reshape(width_row, 3 * width_col)
    columns = lax.all_gather(tile, "col", axis=0, tiled=True)
    block = columns
    proj = lax.psum_scatter(
        jnp.dot(block, flat_w, preferred_element_type=jnp.float32).astype(jnp.bfloat16),
        "row",
        scatter_dimension=0,
        tiled=True,
    )
    padded = with_halo(proj, (("row", 0),), margin)
    after = shifted(upstream_tile[:margin], "row", -1)
    length = rows_dev + 2 * margin
    window = padded.astype(jnp.float32).reshape(length, 3, width_col)
    upstream = jnp.concatenate(
        [
            jnp.zeros((margin, width_col), jnp.float32),
            upstream_tile.astype(jnp.float32),
            after.astype(jnp.float32),
        ],
        axis=0,
    )
    mixed = causal(window, feature_taps)
    query = mixed[:, 0]
    key = mixed[:, 1]
    value = mixed[:, 2]
    product = rounded(key * value)
    inner = causal(product, inner_taps)
    grad_query = upstream * inner
    grad_inner = upstream * query
    grad_product = anticausal(grad_inner, inner_taps)
    grad_mixed = jnp.stack([grad_query, grad_product * value, grad_product * key], axis=1)
    grad_proj = anticausal(grad_mixed, feature_taps)[margin : margin + rows_dev].astype(
        jnp.bfloat16
    )
    gathered = lax.all_gather(grad_proj.reshape(rows_dev, 3 * width_col), "row", axis=0, tiled=True)
    block = gathered
    grad_x = lax.psum_scatter(
        lax.dot_general(
            block, flat_w, (((1,), (1,)), ((), ())), preferred_element_type=jnp.float32
        ).astype(jnp.bfloat16),
        "col",
        scatter_dimension=0,
        tiled=True,
    )
    local = lax.dot_general(
        columns, gathered, (((0,), (0,)), ((), ())), preferred_element_type=jnp.float32
    )
    grad_w = lax.psum(local.astype(jnp.bfloat16), "dp").astype(jnp.float32)
    return (grad_x[None], grad_w.reshape(width_row, 3, width_col))


def solution(mesh):
    placed = (
        P("dp", "col", "row"),
        P("row", None, "col"),
        P(None, None, "col"),
        P(None, "col"),
        P("dp", "row", "col"),
    )
    return jax.shard_map(
        on_device,
        mesh=mesh,
        in_specs=placed,
        out_specs=(P("dp", "col", "row"), P("row", None, "col")),
        check_vma=False,
    )
```

profile of v0, /device:TPU:4, one launch (start us, length us, event | category | flops | bytes accessed | tf_op | source)
XLA Modules:
  0.0 570.4 jit_solution(13624536837322378949)
XLA Ops:
  7.2 0.0 all-gather.6.cloned.1.call-start
  7.2 0.7 all-gather.6.cloned.1.call-update
  7.9 0.0 reduce-scatter.3.cloned.1.call-start
  7.9 1.7 copy.13
  9.7 0.0 copy-start.1
  9.7 72.3 %all-gather.6.cloned.1.call-done = bf16[1,1024,512]{2,1,0:T(8,128)(2,1)} async-done(((bf16[1,128,512]{2,1,0:T(8,128)(2,1)}), bf16[1,1024,512]{2,1,0:T(8,128)(2,1)}) %all-gather.6.cloned.1.call-update) | async-done | bytes 1048592 | tf_op jit(solution)/shard_map/all_gather | solution.py:58
  82.0 4.7 convolution_convert_fusion
  86.7 0.0 copy-done.1
  86.7 0.0 copy-start.3
  86.7 0.0 copy-start.4
  86.7 0.0 copy-start.5
  86.7 0.0 reduce-scatter.3.cloned.1.call-update
  86.7 0.0 all-gather.4.cloned.1.call-start
  86.8 0.8 copy-done.3
  87.6 0.1 copy.11
  87.7 1.3 collective-permute-start
  89.0 0.0 copy-done.4
  89.1 34.9 %reduce-scatter.3.cloned.1.call-done = bf16[128,1536]{1,0:T(8,128)(2,1)} async-done(((bf16[1024,1536]{1,0:T(8,128)(2,1)}), bf16[128,1536]{1,0:T(8,128)(2,1)}) %reduce-scatter.3.cloned.1.call-update) | async-done | bytes 393232 | tf_op jit(solution)/shard_map/reduce_scatter | solution.py:60
  124.0 0.0 copy-start
  124.0 0.8 fusion.6
  124.8 1.3 collective-permute-start.2
  126.1 3.0 collective-permute-start.1
  129.1 0.0 copy-done.5
  129.2 0.0 collective-permute-done
  129.2 1.2 copy.14
  130.5 0.0 collective-permute-done.2
  130.5 0.0 collective-permute-done.1
  130.5 0.0 copy-done
  130.5 0.1 maximum_convert_fusion
  130.6 0.5 copy.21
  131.1 1.6 copy.20
  132.7 0.2 copy.16
  132.9 0.2 copy.15
  133.1 3.2 multiply_add_fusion
  136.3 0.3 fusion.5
  136.6 0.2 slice.174
  136.8 0.2 slice.173
  137.0 0.2 slice.172
  137.2 0.2 slice.171
  137.4 0.2 slice.170
  137.6 0.2 slice.169
  137.8 0.8 multiply_bitcast_fusion.1
  138.6 0.1 multiply_convert_fusion
  139.0 1.8 multiply_bitcast_fusion.2
  140.8 0.1 pad_maximum_fusion
  140.9 0.5 slice.176
  141.4 0.5 slice.175
  141.8 0.0 copy-start.6
  141.8 2.1 fusion.3
  143.9 0.0 all-gather.4.cloned.1.call-update
  143.9 0.0 all-reduce.18.cloned.1.call-start
  144.0 39.6 %all-gather.4.cloned.1.call-done = bf16[1024,1536]{0,1:T(8,128)(2,1)} async-done(((bf16[128,1536]{0,1:T(8,128)(2,1)}), bf16[1024,1536]{0,1:T(8,128)(2,1)}) %all-gather.4.cloned.1.call-update) | async-done | bytes 3145744 | tf_op jit(solution)/shard_map/all_gather | solution.py:91
  183.5 0.0 copy-done.6
  183.5 3.7 convolution_convert_fusion.1
  187.2 1.6 copy.19
  188.8 0.0 copy-start.2
  188.8 0.0 all-reduce.18.cloned.1.call-update
  188.8 0.0 reduce-scatter.5.cloned.1.call-start
  188.9 1.3 copy-done.2
  190.2 4.7 convolution_convert_fusion.2
  194.9 0.0 reduce-scatter.5.cloned.1.call-update
  194.9 294.7 %all-reduce.18.cloned.1.call-done = bf16[512,3,512]{2,0,1:T(8,128)(2,1)} async-done(((bf16[512,3,512]{2,0,1:T(8,128)(2,1)}), bf16[512,3,512]{2,0,1:T(8,128)(2,1)}) %all-reduce.18.cloned.1.call-update) | async-done | bytes 1572880 | tf_op jit(solution)/shard_map/psum | solution.py:104
  489.6 3.5 reshape.28
  493.1 70.8 %reduce-scatter.5.cloned.1.call-done = bf16[128,512]{1,0:T(8,128)(2,1)} async-done(((bf16[1024,512]{1,0:T(8,128)(2,1)}), bf16[128,512]{1,0:T(8,128)(2,1)}) %reduce-scatter.5.cloned.1.call-update) | async-done | bytes 131088 | tf_op jit(solution)/shard_map/reduce_scatter | solution.py:93
  (13 shorter events, 0.3 us)
Async XLA Ops:
  7.2 74.8 %all-gather.6.cloned.1.call-start = ((), (), s32[]{:S(2)}) async-start(), calls=%async_computation.6 | async-start | bytes 1179648 | tf_op jit(solution)/shard_map/all_gather | solution.py:58
  7.9 116.1 %reduce-scatter.3.cloned.1.call-start = ((), (), s32[]{:S(2)}) async-start(), calls=%async_computation.2 | async-start | bytes 3538944 | tf_op jit(solution)/shard_map/reduce_scatter | solution.py:60
  9.7 77.0 %copy-start.1 = (bf16[512,3,512]{0,2,1:T(8,128)(2,1)}, bf16[512,3,512]{0,2,1:T(8,128)(2,1)S(1)}, u32[]{:S(2)}) copy-start(bf16[512,3,512]{0,2,1:T(8,128)(2,1)S(1)} %copy.13) | copy-start | bytes 4718596
  86.7 0.9 copy-start.3
  86.7 2.3 copy-start.4
  86.7 42.5 %copy-start.5 = (f32[7,512]{1,0:T(8,128)S(1)}, f32[7,512]{1,0:T(8,128)}, u32[]{:S(2)}) copy-start(f32[7,512]{1,0:T(8,128)} %param.8) | copy-start | bytes 43012
  86.7 96.8 %all-gather.4.cloned.1.call-start = ((), (), s32[]{:S(2)}) async-start(), calls=%async_computation.3 | async-start | bytes 3538944 | tf_op jit(solution)/shard_map/all_gather | solution.py:91
  87.7 41.5 %collective-permute-start = (bf16[8,512]{0,1:T(8,128)(2,1)S(1)}, bf16[8,512]{0,1:T(8,128)(2,1)S(1)}, u32[]{:S(2)}, u32[]{:S(2)}) collective-permute-start(bf16[8,512]{0,1:T(8,128)(2,1)S(1)} %slice_bitcast_fusion.3), channel_id=1, source_target_pairs={{8,0},{16,8},{24,16},{32,24},{40,32},{48,40},{56,48},{9,1},{17,9},... | collective-permute-start | bytes 24584 | tf_op jit(solution)/shard_map/ppermute | solution.py:27
  124.0 6.5 %copy-start = (bf16[128,1536]{1,0:T(8,128)(2,1)S(1)}, bf16[128,1536]{1,0:T(8,128)(2,1)}, u32[]{:S(2)}) copy-start(bf16[128,1536]{1,0:T(8,128)(2,1)} %reduce-scatter.3.cloned.1.call-done) | copy-start | bytes 1179652
  124.8 5.6 collective-permute-start.2
  126.1 4.4 collective-permute-start.1
  141.8 41.7 %copy-start.6 = (bf16[1,1024,512]{2,1,0:T(8,128)(2,1)S(1)}, bf16[1,1024,512]{2,1,0:T(8,128)(2,1)}, u32[]{:S(2)}) copy-start(bf16[1,1024,512]{2,1,0:T(8,128)(2,1)} %all-gather.6.cloned.1.call-done) | copy-start | bytes 3145732
  143.9 345.7 %all-reduce.18.cloned.1.call-start = ((), (), s32[]{:S(2)}) async-start(), calls=%async_computation.5 | async-start | bytes 3145728 | tf_op jit(solution)/shard_map/psum | solution.py:104
  188.8 1.4 copy-start.2
  188.8 375.0 %reduce-scatter.5.cloned.1.call-start = ((), (), s32[]{:S(2)}) async-start(), calls=%async_computation.4 | async-start | bytes 1179648 | tf_op jit(solution)/shard_map/reduce_scatter | solution.py:93
Sparse Core Ops, SparseCore 0:
  10.1 71.8 all-gather.5
  86.8 37.1 reduce-scatter.2
  144.0 39.4 all-gather.3
  188.9 300.5 all-reduce.17
  492.8 70.9 reduce-scatter.4
where the time goes:
time: 571 us; the launch traced here: 570 us
  waiting for transfers between devices  513 us (90%)
  between operations  14.1 us (2%)
  matrix products  13.1 us (2%)
  local copies, waits for them, and re-layouts  12.5 us (2%)
  other arithmetic  11.9 us (2%)
  starting transfers between devices  5.8 us (1%)
    psum x1, waiting for transfers between devices, on_device(): grad_w = lax.psum(local.astype(jnp.bfloat16), 'dp').astype(jnp.float32)  295 us
    all_gather x1, waiting for transfers between devices, on_device(): columns = lax.all_gather(tile, 'col', axis=0, tiled=True)  72.3 us
    reduce_scatter x1, waiting for transfers between devices, on_device(): lax.psum_scatter(lax.dot_general(block, flat_w, (((1,), (1,)), ((), ())),...  70.8 us
    all_gather x1, waiting for transfers between devices, on_device(): lax.all_gather(grad_proj.reshape(rows_dev, 3 * width_col), 'row', axis=0,...  39.6 us
    reduce_scatter x1, waiting for transfers between devices, on_device(): lax.psum_scatter(jnp.dot(block, flat_w, preferred_element_type=jnp.float3...  34.9 us
  transfers between devices with their start and end apart: 8, of which 5 were waited for; matrix products, arithmetic and copies ran while one was open for 2% of the time, Pallas kernels for 0%

commit v1 on v0

--- a/solution.py
+++ b/solution.py
@@ -101,7 +101,8 @@
     local = lax.dot_general(
         columns, gathered, (((0,), (0,)), ((), ())), preferred_element_type=jnp.float32
     )
-    grad_w = lax.psum(local.astype(jnp.bfloat16), "dp").astype(jnp.float32)
+    _answer_ends = lambda sample, row_axis: jnp.sum(lax.all_gather(sample, row_axis), axis=0)
+    grad_w = _answer_ends(local.astype(jnp.bfloat16), "dp").astype(jnp.float32)
     return (grad_x[None], grad_w.reshape(width_row, 3, width_col))
 
 

time: 571 us -> 700 us (1.23)
  the two profiles are of different devices: /device:TPU:4 before, /device:TPU:6 now
where the time goes in v1:
time: 700 us; the launch traced here: 699 us
  waiting for transfers between devices  625 us (89%)
  local copies, waits for them, and re-layouts  22.2 us (3%)
  other arithmetic  17.8 us (3%)
  matrix products  14.2 us (2%)
  between operations  14.1 us (2%)
    all_gather x1, waiting for transfers between devices, on_device(): lax.all_gather(sample, row_axis)  416 us
    all_gather x1, waiting for transfers between devices, on_device(): columns = lax.all_gather(tile, 'col', axis=0, tiled=True)  72.3 us
    reduce_scatter x1, waiting for transfers between devices, on_device(): lax.psum_scatter(lax.dot_general(block, flat_w, (((1,), (1,)), ((), ())),...  61.7 us
    all_gather x1, waiting for transfers between devices, on_device(): lax.all_gather(grad_proj.reshape(rows_dev, 3 * width_col), 'row', axis=0,...  39.6 us
    reduce_scatter x1, waiting for transfers between devices, on_device(): lax.psum_scatter(jnp.dot(block, flat_w, preferred_element_type=jnp.float3...  34.9 us
    unnamed x18, local copies, waits for them, and re-layouts  15.3 us
  transfers between devices with their start and end apart: 8, of which 5 were waited for; matrix products, arithmetic and copies ran while one was open for 4% of the time, Pallas kernels for 0%

profile of v1, /device:TPU:6, one launch (start us, length us, event | category | flops | bytes accessed | tf_op | source)
XLA Modules:
  0.0 699.2 jit_solution(11496303833266075919)
XLA Ops:
  7.2 0.0 all-gather.8.cloned.1.call-start
  7.2 0.7 all-gather.8.cloned.1.call-update
  7.9 0.0 reduce-scatter.3.cloned.1.call-start
  7.9 1.7 copy.12
  9.7 0.0 copy-start.1
  9.7 72.3 %all-gather.8.cloned.1.call-done = bf16[1,1024,512]{2,1,0:T(8,128)(2,1)} async-done(((bf16[1,128,512]{2,1,0:T(8,128)(2,1)}), bf16[1,1024,512]{2,1,0:T(8,128)(2,1)}) %all-gather.8.cloned.1.call-update) | async-done | bytes 1048592 | tf_op jit(solution)/shard_map/all_gather | solution.py:58
  81.9 4.7 convolution_convert_fusion
  86.7 0.0 copy-done.1
  86.7 0.0 copy-start.3
  86.7 0.0 copy-start.4
  86.7 0.0 copy-start.5
  86.7 0.0 reduce-scatter.3.cloned.1.call-update
  86.7 0.0 all-gather.6.cloned.1.call-start
  86.8 0.8 copy-done.3
  87.6 0.1 copy.10
  87.7 1.3 collective-permute-start
  89.0 0.0 copy-done.4
  89.1 34.9 %reduce-scatter.3.cloned.1.call-done = bf16[128,1536]{1,0:T(8,128)(2,1)} async-done(((bf16[1024,1536]{1,0:T(8,128)(2,1)}), bf16[128,1536]{1,0:T(8,128)(2,1)}) %reduce-scatter.3.cloned.1.call-update) | async-done | bytes 393232 | tf_op jit(solution)/shard_map/reduce_scatter | solution.py:60
  124.0 0.0 copy-start
  124.0 0.8 fusion.7
  124.8 1.3 collective-permute-start.2
  126.1 3.0 collective-permute-start.1
  129.1 0.0 copy-done.5
  129.2 0.0 collective-permute-done
  129.2 1.2 copy.13
  130.4 0.0 collective-permute-done.2
  130.4 0.0 collective-permute-done.1
  130.5 0.0 copy-done
  130.5 0.1 maximum_convert_fusion
  130.6 0.5 copy.20
  131.0 1.6 copy.19
  132.6 0.2 copy.15
  132.9 0.2 copy.14
  133.1 3.2 multiply_add_fusion
  136.3 0.3 fusion.6
  136.6 0.2 slice.174
  136.8 0.2 slice.173
  137.0 0.2 slice.172
  137.2 0.2 slice.171
  137.4 0.2 slice.170
  137.6 0.2 slice.169
  137.8 0.8 multiply_bitcast_fusion.1
  138.6 0.1 multiply_convert_fusion
  139.0 1.8 multiply_bitcast_fusion.2
  140.7 0.1 pad_maximum_fusion
  140.9 0.5 slice.176
  141.3 0.5 slice.175
  141.8 0.0 copy-start.6
  141.8 2.1 fusion.4
  143.9 0.0 all-gather.6.cloned.1.call-update
  143.9 0.0 all-gather.10.cloned.1.call-start
  144.0 39.6 %all-gather.6.cloned.1.call-done = bf16[1024,1536]{0,1:T(8,128)(2,1)} async-done(((bf16[128,1536]{0,1:T(8,128)(2,1)}), bf16[1024,1536]{0,1:T(8,128)(2,1)}) %all-gather.6.cloned.1.call-update) | async-done | bytes 3145744 | tf_op jit(solution)/shard_map/all_gather | solution.py:91
  183.5 0.0 copy-done.6
  183.5 4.8 fusion
  188.4 0.0 all-gather.10.cloned.1.call-update
  188.4 0.2 reduce-scatter.5.cloned.1.call-start
  188.6 1.2 copy-done.2
  189.8 4.7 convolution_convert_fusion.2
  194.5 0.0 reduce-scatter.5.cloned.1.call-update
  194.5 415.6 %all-gather.10.cloned.1.call-done = bf16[4096,1536]{0,1:T(8,128)(2,1)} async-done(((bf16[512,1536]{0,1:T(8,128)(2,1)}), bf16[4096,1536]{0,1:T(8,128)(2,1)}) %all-gather.10.cloned.1.call-update) | async-done | bytes 12582928 | tf_op jit(solution)/shard_map/all_gather | solution.py:104
  610.1 9.4 %copy.21 = bf16[192,8,8,512]{3,2,1,0:T(8,128)(2,1)S(1)} copy(bf16[192,8,8,512]{3,1,2,0:T(8,128)(2,1)} %bitcast.68) | data formatting | bytes 25165824
  619.5 9.4 %bitcast_reduce_fusion = bf16[512,1536]{0,1:T(8,128)(2,1)S(1)} fusion(bf16[192,8,8,512]{3,2,1,0:T(8,128)(2,1)S(1)} %copy.21), kind=kLoop, calls=%fused_computation | loop fusion | flops 5505024 | bytes 14155776 | tf_op jit(solution)/shard_map/reduce_sum | solution.py:104
  628.9 2.1 copy.18
  631.0 61.7 %reduce-scatter.5.cloned.1.call-done = bf16[128,512]{1,0:T(8,128)(2,1)} async-done(((bf16[1024,512]{1,0:T(8,128)(2,1)}), bf16[128,512]{1,0:T(8,128)(2,1)}) %reduce-scatter.5.cloned.1.call-update) | async-done | bytes 131088 | tf_op jit(solution)/shard_map/reduce_scatter | solution.py:93
  (14 shorter events, 0.3 us)
Async XLA Ops:
  7.2 74.8 %all-gather.8.cloned.1.call-start = ((), (), s32[]{:S(2)}) async-start(), calls=%async_computation.5 | async-start | bytes 1179648 | tf_op jit(solution)/shard_map/all_gather | solution.py:58
  7.9 116.1 %reduce-scatter.3.cloned.1.call-start = ((), (), s32[]{:S(2)}) async-start(), calls=%async_computation.2 | async-start | bytes 3538944 | tf_op jit(solution)/shard_map/reduce_scatter | solution.py:60
  9.7 77.0 %copy-start.1 = (bf16[512,3,512]{0,2,1:T(8,128)(2,1)}, bf16[512,3,512]{0,2,1:T(8,128)(2,1)S(1)}, u32[]{:S(2)}) copy-start(bf16[512,3,512]{0,2,1:T(8,128)(2,1)S(1)} %copy.12) | copy-start | bytes 4718596
  86.7 0.9 copy-start.3
  86.7 2.3 copy-start.4
  86.7 42.5 %copy-start.5 = (f32[7,512]{1,0:T(8,128)S(1)}, f32[7,512]{1,0:T(8,128)}, u32[]{:S(2)}) copy-start(f32[7,512]{1,0:T(8,128)} %param.8) | copy-start | bytes 43012
  86.7 96.8 %all-gather.6.cloned.1.call-start = ((), (), s32[]{:S(2)}) async-start(), calls=%async_computation.3 | async-start | bytes 3538944 | tf_op jit(solution)/shard_map/all_gather | solution.py:91
  87.7 41.5 %collective-permute-start = (bf16[8,512]{0,1:T(8,128)(2,1)S(1)}, bf16[8,512]{0,1:T(8,128)(2,1)S(1)}, u32[]{:S(2)}, u32[]{:S(2)}) collective-permute-start(bf16[8,512]{0,1:T(8,128)(2,1)S(1)} %slice_bitcast_fusion.3), channel_id=1, source_target_pairs={{8,0},{16,8},{24,16},{32,24},{40,32},{48,40},{56,48},{9,1},{17,9},... | collective-permute-start | bytes 24584 | tf_op jit(solution)/shard_map/ppermute | solution.py:27
  124.0 6.5 copy-start
  124.8 5.6 collective-permute-start.2
  126.1 4.4 collective-permute-start.1
  141.8 41.7 %copy-start.6 = (bf16[1,1024,512]{2,1,0:T(8,128)(2,1)S(1)}, bf16[1,1024,512]{2,1,0:T(8,128)(2,1)}, u32[]{:S(2)}) copy-start(bf16[1,1024,512]{2,1,0:T(8,128)(2,1)} %all-gather.8.cloned.1.call-done) | copy-start | bytes 3145732
  143.9 466.2 %all-gather.10.cloned.1.call-start = ((), (), s32[]{:S(2)}) async-start(), calls=%async_computation.6 | async-start | bytes 14155776 | tf_op jit(solution)/shard_map/all_gather | solution.py:104
  188.4 1.4 copy-start.2
  188.4 504.3 %reduce-scatter.5.cloned.1.call-start = ((), (), s32[]{:S(2)}) async-start(), calls=%async_computation.4 | async-start | bytes 1179648 | tf_op jit(solution)/shard_map/reduce_scatter | solution.py:93
Sparse Core Ops, SparseCore 0:
  10.1 71.8 all-gather.7
  86.8 37.1 reduce-scatter.2
  144.0 39.4 all-gather.5
  188.5 421.5 all-gather.9
  613.3 79.3 reduce-scatter.4
